TPU v7x, 256 devices: a whole 4x4x8 slice. The times are simulated.
256 devices in a mesh: dom: 32 (over y_hi, z, core), hid: 8 (over y_lo, x).
Axes of the slice: x: 4, y: 4 (y_hi: 2, y_lo: 2; y = y_hi * 2 + y_lo), z: 8, core: 2. Of those that a mesh axis runs over, the one named last changes fastest.
Arguments:
- features: bfloat16 [512, 32768], P(None, 'dom'), may hold values from -6 to 6
- weight: bfloat16 [512, 512], P(None, 'hid'), may hold values from -0.25 to 0.25
- band_tiles: bfloat16 [3072, 32768], P(None, 'dom'), may hold values from -0.109375 to 0.109375
- tile_live: int32 [12, 128], P(None, 'dom'), may hold values 0 or 1
- send_rows: int32 [32, 32, 128], P('dom'), may hold values from 0 to 1023
- recv_rows: int32 [32, 32, 128], P('dom'), may hold values from 0 to 1023
- edge_weight: float32 [32, 32, 128], P('dom'), may hold values from 0.25 to 1
- live_slots: int32 [32, 32], P('dom'), may hold values from 96 to 128, as said below
- bias_terms: float32 [512], P('hid'), may hold values from -3 to 3
- cotangent: bfloat16 [512, 32768], P('hid', 'dom'), may hold values from -6 to 6
Outputs:
- output: bfloat16 [512, 32768], P('hid', 'dom')
- feature_grad: bfloat16 [512, 32768], P('hid', 'dom')
- weight_grad: float32 [512, 512], P(None, 'hid')
- bias_grad: float32 [512], P('hid')
Inputs may be any that keep to these rules, and one draw needn't show every extreme that they name: `live_slots`: every reader block has at least one owner block whose list has all 128 slots live.
All inputs are finite; a program needn't handle non-finite values. No bound on the sum of `tile_live` on one device may be relied on, other than what follows from the above.
Results may differ from a plain program's by a relative error of at most 0.0065.
Values may be sent and summed in bfloat16 or wider, within the bound.
A program may use at most 64 MiB of HBM per device.

v0:
```python
import jax
import jax.numpy as jnp
from jax import lax
from jax.sharding import PartitionSpec as P

TILE = 256


def passed_along(block, axis, distance):
    devices = range(lax.axis_size(axis))
    route = [((i - distance) % len(devices), i) for i in devices]
    return lax.ppermute(block, axis, route)


def silu_grad(value):
    gate = jax.nn.sigmoid(value)
    return gate * (1.0 + value * (1.0 - gate))


def on_device(
    features,
    weight,
    band_tiles,
    tile_live,
    send_rows,
    recv_rows,
    edge_weight,
    live_slots,
    bias_terms,
    cotangent,
):
    row_count = features.shape[1]
    local_width = weight.shape[1]
    mapped = lax.dot_general(
        weight, features, (((0,), (0,)), ((), ())), preferred_element_type=jnp.float32
    ).astype(jnp.bfloat16)
    tile_mask = tile_live.astype(jnp.bfloat16)
    dense = (
        band_tiles.reshape(3 * row_count // TILE, TILE, row_count // TILE, TILE)
        * tile_mask[:, None, :, None]
    ).reshape(3 * row_count, row_count)
    summed = jnp.dot(mapped, dense[row_count : 2 * row_count], preferred_element_type=jnp.float32)
    for offset in (0, 2):
        arrived = passed_along(mapped, "dom", 1 - offset)
        summed = summed + jnp.dot(
            arrived,
            dense[offset * row_count : (offset + 1) * row_count],
            preferred_element_type=jnp.float32,
        )
    slot_ids = jnp.arange(send_rows.shape[2])
    slot_weight = edge_weight[0] * (slot_ids[None, :] < live_slots[0][:, None]).astype(jnp.float32)
    outgoing = mapped[:, send_rows[0]]
    incoming = lax.all_to_all(outgoing, "dom", split_axis=1, concat_axis=1, tiled=True)
    weighted = incoming.astype(jnp.float32) * slot_weight[None]
    summed = summed.at[:, recv_rows[0].reshape(-1)].add(weighted.reshape(local_width, -1))
    act = summed + bias_terms[:, None]
    output = jax.nn.silu(act).astype(jnp.bfloat16)
    pre_grad = (cotangent.astype(jnp.float32) * silu_grad(act)).astype(jnp.bfloat16)
    contract = (((1,), (1,)), ((), ()))
    map_grad = lax.dot_general(
        pre_grad, dense[row_count : 2 * row_count], contract, preferred_element_type=jnp.float32
    )
    for offset in (0, 2):
        term = lax.dot_general(
            pre_grad,
            dense[offset * row_count : (offset + 1) * row_count],
            contract,
            preferred_element_type=jnp.float32,
        )
        map_grad = map_grad + passed_along(term, "dom", offset - 1)
    message = (pre_grad.astype(jnp.float32)[:, recv_rows[0]] * slot_weight[None]).astype(
        jnp.bfloat16
    )
    returned = lax.all_to_all(message, "dom", split_axis=1, concat_axis=1, tiled=True)
    map_grad = map_grad.at[:, send_rows[0].reshape(-1)].add(
        returned.astype(jnp.float32).reshape(local_width, -1)
    )
    grad_b = map_grad.astype(jnp.bfloat16)
    weight_part = lax.dot_general(features, grad_b, contract, preferred_element_type=jnp.float32)
    bias_part = jnp.sum(pre_grad.astype(jnp.float32), axis=1)
    weight_grad, bias_grad = lax.psum((weight_part, bias_part), "dom")
    feature_grad = lax.psum_scatter(
        jnp.dot(weight, grad_b, preferred_element_type=jnp.float32),
        "hid",
        scatter_dimension=0,
        tiled=True,
    ).astype(jnp.bfloat16)
    return (output, feature_grad, weight_grad, bias_grad)


def solution(mesh):
    return jax.shard_map(
        on_device,
        mesh=mesh,
        in_specs=(
            P(None, "dom"),
            P(None, "hid"),
            P(None, "dom"),
            P(None, "dom"),
            P("dom", None, None),
            P("dom", None, None),
            P("dom", None, None),
            P("dom", None),
            P("hid"),
            P("hid", "dom"),
        ),
        out_specs=(P("hid", "dom"), P("hid", "dom"), P(None, "hid"), P("hid")),
        check_vma=False,
    )
```

profile of v0, /device:TPU:2, one launch (start us, length us, event | category | flops | bytes accessed | tf_op | source)
XLA Modules:
  0.0 441.8 jit_solution(8998535476931524258)
XLA Ops:
  8.0 1.2 copy-done
  9.2 1.1 convolution_convert_fusion
  10.5 8.0 %collective-permute-start.1 = (bf16[64,1024]{1,0:T(8,128)(2,1)S(1)}, bf16[64,1024]{1,0:T(8,128)(2,1)}, u32[]{:S(2)}, u32[]{:S(2)}) collective-permute-start(bf16[64,1024]{1,0:T(8,128)(2,1)S(1)} %convolution_convert_fusion), channel_id=1, source_target_pairs={{8,0},{16,8},{24,16},{32,24},{40,32},{48,40},{56,48},{64,56},{72,6... | collective-permute-start | bytes 393224 | tf_op jit(solution)/shard_map/ppermute | solution.py:12
  19.4 12.1 %gather_fusion = bf16[4096,64]{1,0:T(8,128)(2,1)S(1)} fusion(bf16[64,1024]{0,1:T(8,128)(2,1)S(1)} %copy.31, s32[4096]{0:T(1024)S(1)} %fusion.6), kind=kCustom, calls=%fused_computation | custom fusion | bytes 1064960 | tf_op jit(solution)/shard_map/gather | solution.py:52
  32.6 6.6 %all-to-all-start = ((bf16[64,32,128]{2,0,1:T(8,128)(2,1)}), bf16[64,32,128]{2,0,1:T(8,128)(2,1)}, u32[]{:S(2)}, u32[]{:S(2)}) async-start(bf16[64,32,128]{2,0,1:T(8,128)(2,1)} %bitcast.5), calls=%async_computation | async-start | bytes 1048576 | tf_op jit(solution)/shard_map/all_to_all | solution.py:53
  39.2 11.2 %reshape.173 = bf16[12,256,4,256]{3,2,1,0:T(4,128)(2,1)} reshape(bf16[3072,1024]{1,0:T(8,128)(2,1)} %param.12) | data formatting | bytes 12582912 | tf_op jit(solution)/shard_map/reshape | solution.py:39
  50.5 8.2 %broadcast_multiply_fusion = bf16[12,256,4,256]{3,2,1,0:T(4,128)(2,1)} fusion(bf16[12,256,4,256]{3,2,1,0:T(4,128)(2,1)} %reshape.173, bf16[12,4]{1,0:T(8,128)(2,1)S(1)} %copy.30), kind=kLoop, calls=%fused_computation.4 | loop fusion | flops 3145728 | bytes 12583008 | tf_op jit(solution)/shard_map/mul | solution.py:39
  58.6 4.1 fusion.9
  64.5 2.0 copy.49
  67.2 1.8 copy.36
  69.9 1.3 fusion.8
  71.2 1.4 convolution_add_fusion.2
  72.6 1.4 fusion.1
  75.4 1.9 copy.35
  77.3 23.1 %scatter_fusion = f32[64,1024]{0,1:T(8,128)S(1)} fusion(f32[64,1024]{0,1:T(8,128)S(1)} %copy.34, s32[4096]{0:T(1024)S(1)} %bitcast.79, f32[4096,64]{1,0:T(8,128)} %copy.35), kind=kCustom, calls=%fused_computation.2 | custom fusion | flops 262144 | bytes 3162112 | tf_op jit(solution)/shard_map/scatter-add | solution.py:55
  101.4 3.1 fusion.11
  104.4 1.5 fusion.12
  106.0 5.2 %collective-permute-start.2 = (f32[64,1024]{1,0:T(8,128)}, f32[64,1024]{1,0:T(8,128)}, u32[]{:S(2)}, u32[]{:S(2)}) collective-permute-start(f32[64,1024]{1,0:T(8,128)} %fusion.11), channel_id=1, source_target_pairs={{8,0},{16,8},{24,16},{32,24},{40,32},{48,40},{56,48},{64,56},{72,6... | collective-permute-start | bytes 786440 | tf_op jit(solution)/shard_map/ppermute | solution.py:12
  111.2 14.2 %gather_fusion.1 = f32[4096,64]{1,0:T(8,128)} fusion(f32[64,1024]{0,1:T(8,128)S(1)} %convert_element_type.39, s32[4096]{0:T(1024)S(1)} %copy-done.9), kind=kCustom, calls=%fused_computation.1 | custom fusion | bytes 2113536 | tf_op jit(solution)/shard_map/gather | solution.py:71
  125.4 3.1 copy.37
  128.5 2.3 fusion.2
  130.8 7.1 %all-to-all-start.1 = ((bf16[64,32,128]{2,0,1:T(8,128)(2,1)}), bf16[64,32,128]{2,0,1:T(8,128)(2,1)}, u32[]{:S(2)}, u32[]{:S(2)}) async-start(bf16[64,32,128]{2,0,1:T(8,128)(2,1)} %fusion.2), calls=%async_computation.1 | async-start | bytes 1048576 | tf_op jit(solution)/shard_map/all_to_all | solution.py:74
  138.1 2.5 fusion
  140.6 1.1 copy.39
  141.8 16.1 %all-to-all-done.1 = bf16[64,32,128]{2,0,1:T(8,128)(2,1)} async-done(((bf16[64,32,128]{2,0,1:T(8,128)(2,1)}), bf16[64,32,128]{2,0,1:T(8,128)(2,1)}, u32[]{:S(2)}, u32[]{:S(2)}) %all-to-all-start.1) | async-done | bytes 524320 | tf_op jit(solution)/shard_map/all_to_all | solution.py:74
  159.0 1.9 copy.40
  160.9 22.9 %scatter_fusion.1 = f32[64,1024]{0,1:T(8,128)S(1)} fusion(f32[64,1024]{0,1:T(8,128)S(1)} %copy.39, s32[4096]{0:T(1024)S(1)} %bitcast.80, f32[4096,64]{1,0:T(8,128)} %copy.40), kind=kCustom, calls=%fused_computation.3 | custom fusion | flops 262144 | bytes 3162112 | tf_op jit(solution)/shard_map/scatter-add | solution.py:75
  183.8 1.7 convolution_bitcast_fusion
  185.6 2.9 copy.43
  190.5 65.5 %psum.15 = f32[64]{0:T(128)} all-reduce(f32[64]{0:T(128)S(1)} %get-tuple-element.16), channel_id=1, replica_groups=mesh['dom'=32,'hid'=8] {'dom'}, use_global_device_ids=true, to_apply=%region_5.6 | all-reduce | flops 64 | bytes 512 | tf_op jit(solution)/shard_map/psum | solution.py:81
  257.9 174.9 %all-reduce.2.cloned.1.call-done = f32[512,64]{0,1:T(8,128)} async-done(((f32[512,64]{0,1:T(8,128)}), f32[512,64]{0,1:T(8,128)}) %all-reduce.2.cloned.1.call-update) | async-done | bytes 131088 | tf_op jit(solution)/shard_map/psum | solution.py:81
  432.8 1.6 copy.55
  (59 shorter events, 13.0 us)
Async XLA Ops:
  8.0 1.2 copy-start
  10.4 60.8 %collective-permute-start = (bf16[64,1024]{1,0:T(8,128)(2,1)S(1)}, bf16[64,1024]{1,0:T(8,128)(2,1)}, u32[]{:S(2)}, u32[]{:S(2)}) collective-permute-start(bf16[64,1024]{1,0:T(8,128)(2,1)S(1)} %convolution_convert_fusion), channel_id=1, source_target_pairs={{248,0},{0,8},{8,16},{16,24},{24,32},{32,40},{40,48},{48,56},{56,6... | collective-permute-start | bytes 393224 | tf_op jit(solution)/shard_map/ppermute | solution.py:12
  10.5 62.2 %collective-permute-start.1 = (bf16[64,1024]{1,0:T(8,128)(2,1)S(1)}, bf16[64,1024]{1,0:T(8,128)(2,1)}, u32[]{:S(2)}, u32[]{:S(2)}) collective-permute-start(bf16[64,1024]{1,0:T(8,128)(2,1)S(1)} %convolution_convert_fusion), channel_id=1, source_target_pairs={{8,0},{16,8},{24,16},{32,24},{40,32},{48,40},{56,48},{64,56},{72,6... | collective-permute-start | bytes 393224 | tf_op jit(solution)/shard_map/ppermute | solution.py:12
  32.6 41.6 %all-to-all-start = ((bf16[64,32,128]{2,0,1:T(8,128)(2,1)}), bf16[64,32,128]{2,0,1:T(8,128)(2,1)}, u32[]{:S(2)}, u32[]{:S(2)}) async-start(bf16[64,32,128]{2,0,1:T(8,128)(2,1)} %bitcast.5), calls=%async_computation | async-start | bytes 1048576 | tf_op jit(solution)/shard_map/all_to_all | solution.py:53
  39.2 11.2 %copy-start.13 = (s32[12,4]{0,1:T(4,128)S(1)}, s32[12,4]{0,1:T(4,128)}, u32[]{:S(2)}) copy-start(s32[12,4]{0,1:T(4,128)} %param.13) | copy-start | bytes 580
  63.2 1.3 copy-start.4
  64.5 6.7 %copy-start.1 = (bf16[128,8,4,256]{3,1,2,0:T(8,128)(2,1)}, bf16[128,8,4,256]{3,1,2,0:T(8,128)(2,1)S(1)}, u32[]{:S(2)}) copy-start(bf16[128,8,4,256]{3,1,2,0:T(8,128)(2,1)S(1)} %copy.48) | copy-start | bytes 6291460
  64.5 2.0 copy-start.11
  68.9 3.7 copy-start.2
  74.2 3.1 copy-start.10
  77.3 23.1 %copy-start.7 = (bf16[64,1024]{0,1:T(8,128)(2,1)S(1)}, bf16[64,1024]{0,1:T(8,128)(2,1)}, u32[]{:S(2)}) copy-start(bf16[64,1024]{0,1:T(8,128)(2,1)} %copy.36) | copy-start | bytes 393220
  100.4 4.1 copy-start.3
  104.4 6.8 %copy-start.9 = (s32[4096]{0:T(1024)S(1)}, s32[4096]{0:T(1024)}, u32[]{:S(2)}) copy-start(s32[4096]{0:T(1024)} %fusion.8) | copy-start | bytes 49156
  106.0 32.1 %collective-permute-start.2 = (f32[64,1024]{1,0:T(8,128)}, f32[64,1024]{1,0:T(8,128)}, u32[]{:S(2)}, u32[]{:S(2)}) collective-permute-start(f32[64,1024]{1,0:T(8,128)} %fusion.11), channel_id=1, source_target_pairs={{8,0},{16,8},{24,16},{32,24},{40,32},{48,40},{56,48},{64,56},{72,6... | collective-permute-start | bytes 786440 | tf_op jit(solution)/shard_map/ppermute | solution.py:12
  111.2 26.9 %collective-permute-start.3 = (f32[64,1024]{1,0:T(8,128)}, f32[64,1024]{1,0:T(8,128)}, u32[]{:S(2)}, u32[]{:S(2)}) collective-permute-start(f32[64,1024]{1,0:T(8,128)} %fusion.12), channel_id=1, source_target_pairs={{248,0},{0,8},{8,16},{16,24},{24,32},{32,40},{40,48},{48,56},{56,6... | collective-permute-start | bytes 786440 | tf_op jit(solution)/shard_map/ppermute | solution.py:12
  128.5 9.5 %copy-start.12 = (s32[1,32,128]{2,1,0:T(8,128)S(1)}, s32[1,32,128]{2,1,0:T(8,128)}, u32[]{:S(2)}) copy-start(s32[1,32,128]{2,1,0:T(8,128)} %param.14) | copy-start | bytes 49156
  128.5 9.6 %copy-start.5 = (bf16[128,8,4,256]{3,1,2,0:T(8,128)(2,1)S(1)}, bf16[128,8,4,256]{3,1,2,0:T(8,128)(2,1)}, u32[]{:S(2)}) copy-start(bf16[128,8,4,256]{3,1,2,0:T(8,128)(2,1)} %copy-done.4) | copy-start | bytes 6291460
  130.8 27.1 %all-to-all-start.1 = ((bf16[64,32,128]{2,0,1:T(8,128)(2,1)}), bf16[64,32,128]{2,0,1:T(8,128)(2,1)}, u32[]{:S(2)}, u32[]{:S(2)}) async-start(bf16[64,32,128]{2,0,1:T(8,128)(2,1)} %fusion.2), calls=%async_computation.1 | async-start | bytes 1048576 | tf_op jit(solution)/shard_map/all_to_all | solution.py:74
  138.0 118.0 %reduce-scatter.4.cloned.1.call-start = ((), (), s32[]{:S(2)}) async-start(), calls=%async_computation.4 | async-start | bytes 2359296
  160.9 22.9 %copy-start.8 = (bf16[512,64]{0,1:T(8,128)(2,1)S(1)}, bf16[512,64]{0,1:T(8,128)(2,1)}, u32[]{:S(2)}) copy-start(bf16[512,64]{0,1:T(8,128)(2,1)} %param.11) | copy-start | bytes 196612
  188.5 1.2 copy-start.6
  188.5 244.3 %all-reduce.2.cloned.1.call-start = ((), (), s32[]{:S(2)}) async-start(), calls=%async_computation.3 | async-start | bytes 262144 | tf_op jit(solution)/shard_map/psum | solution.py:81
Sparse Core Ops, SparseCore 0:
  188.6 36.9 reduce-scatter.3
Sparse Core Ops, SparseCore 1:
  192.2 240.6 all-reduce.1
where the time goes:
time: 443 us; the launch traced here: 442 us
  waiting for transfers between devices  191 us (43%)
  blocking collectives  65.5 us (15%)
  local copies, waits for them, and re-layouts  64.8 us (15%)
  other arithmetic  63.3 us (14%)
  starting transfers between devices  27.1 us (6%)
  between operations  15.8 us (4%)
  matrix products  14.3 us (3%)
    psum x1, waiting for transfers between devices, on_device(): weight_grad, bias_grad = lax.psum((weight_part, bias_part), 'dom')  175 us
    psum x1, blocking collectives, on_device(): weight_grad, bias_grad = lax.psum((weight_part, bias_part), 'dom')  65.5 us
    scatter-add x1, other arithmetic, on_device(): summed.at[:, recv_rows[0].reshape(-1)]  23.1 us
    scatter-add x1, other arithmetic, on_device(): map_grad.at[:, send_rows[0].reshape(-1)]  22.9 us
    gather x2, local copies, waits for them, and re-layouts, on_device(): pre_grad.astype(jnp.float32)[:, recv_rows[0]] * slot_weight[None]  17.3 us
    all_to_all x1, waiting for transfers between devices, on_device(): lax.all_to_all(message, 'dom', split_axis=1, concat_axis=1, tiled=True)  16.1 us
    unnamed x37, local copies, waits for them, and re-layouts  13.5 us
    ppermute x4, starting transfers between devices, passed_along(): return lax.ppermute(block, axis, route)  13.3 us
  transfers between devices with their start and end apart: 8, of which 2 were waited for; matrix products, arithmetic and copies ran while one was open for 17% of the time, Pallas kernels for 0%

commit v1 on v0

--- a/solution.py
+++ b/solution.py
@@ -71,7 +71,11 @@
     message = (pre_grad.astype(jnp.float32)[:, recv_rows[0]] * slot_weight[None]).astype(
         jnp.bfloat16
     )
-    returned = lax.all_to_all(message, "dom", split_axis=1, concat_axis=1, tiled=True)
+    frame_out = lax.axis_size("dom")
+    far_arr = jnp.split(message, frame_out, axis=1)
+    val2 = jnp.stack(far_arr, axis=0)
+    fresh = lax.all_to_all(val2, axis_name="dom", split_axis=0, concat_axis=0)
+    returned = jnp.concatenate(fresh, axis=1)
     map_grad = map_grad.at[:, send_rows[0].reshape(-1)].add(
         returned.astype(jnp.float32).reshape(local_width, -1)
     )

time: 443 us -> 464 us (1.047)
  local copies, waits for them, and re-layouts: 64.8 us -> 85.9 us
    unnamed x37 -> x73, local copies, waits for them, and re-layouts: 13.5 us -> 33.4 us
    all_to_all x1, waiting for transfers between devices: 16.1 us -> 0.01 us  [on_device(): fresh = lax.all_to_all(val2, axis_name='dom', split_axis=0, concat_axis=0)]
    ppermute x4, waiting for transfers between devices: 0.01 us -> 15.2 us  [passed_along(): return lax.ppermute(block, axis, route)]
  transfers between devices with their start and end apart: 8 -> 8, of which waited for: 2 -> 3; matrix products, arithmetic and copies ran while one was open for 17% -> 12% of each run, Pallas kernels for 0% -> 0%
where the time goes in v1:
time: 464 us; the launch traced here: 463 us
  waiting for transfers between devices  192 us (41%)
  local copies, waits for them, and re-layouts  85.9 us (19%)
  blocking collectives  65.5 us (14%)
  other arithmetic  61.7 us (13%)
  starting transfers between devices  29.8 us (6%)
  between operations  15.8 us (3%)
  matrix products  12.5 us (3%)
    psum x1, waiting for transfers between devices, on_device(): weight_grad, bias_grad = lax.psum((weight_part, bias_part), 'dom')  177 us
    psum x1, blocking collectives, on_device(): weight_grad, bias_grad = lax.psum((weight_part, bias_part), 'dom')  65.5 us
    unnamed x73, local copies, waits for them, and re-layouts  33.4 us
    scatter-add x1, other arithmetic, on_device(): summed.at[:, recv_rows[0].reshape(-1)]  23.1 us
    scatter-add x1, other arithmetic, on_device(): map_grad.at[:, send_rows[0].reshape(-1)]  22.9 us
    gather x2, local copies, waits for them, and re-layouts, on_device(): pre_grad.astype(jnp.float32)[:, recv_rows[0]] * slot_weight[None]  17.3 us
    ppermute x4, waiting for transfers between devices, passed_along(): return lax.ppermute(block, axis, route)  15.2 us
    ppermute x4, starting transfers between devices, passed_along(): return lax.ppermute(block, axis, route)  13.3 us
  transfers between devices with their start and end apart: 8, of which 3 were waited for; matrix products, arithmetic and copies ran while one was open for 12% of the time, Pallas kernels for 0%

profile of v1, /device:TPU:2, one launch (start us, length us, event | category | flops | bytes accessed | tf_op | source)
XLA Modules:
  0.0 463.3 jit_solution(15642863931123043049)
XLA Ops:
  8.0 1.2 copy-done
  10.5 8.0 %collective-permute-start.1 = (bf16[64,1024]{1,0:T(8,128)(2,1)S(1)}, bf16[64,1024]{1,0:T(8,128)(2,1)S(1)}, u32[]{:S(2)}, u32[]{:S(2)}) collective-permute-start(bf16[64,1024]{1,0:T(8,128)(2,1)S(1)} %convolution_convert_fusion), channel_id=1, source_target_pairs={{8,0},{16,8},{24,16},{32,24},{40,32},{48,40},{56,48},{64,56},{72,6... | collective-permute-start | bytes 393224 | tf_op jit(solution)/shard_map/ppermute | solution.py:12
  18.6 1.4 fusion.6
  20.0 12.1 %gather_fusion = bf16[4096,64]{1,0:T(8,128)(2,1)S(1)} fusion(bf16[64,1024]{0,1:T(8,128)(2,1)S(1)} %copy.31, s32[4096]{0:T(1024)S(1)} %get-tuple-element.22), kind=kCustom, calls=%fused_computation | custom fusion | bytes 1064960 | tf_op jit(solution)/shard_map/gather | solution.py:52
  33.3 6.6 %all-to-all-start = ((bf16[64,32,128]{2,0,1:T(8,128)(2,1)}), bf16[64,32,128]{2,0,1:T(8,128)(2,1)}, u32[]{:S(2)}, u32[]{:S(2)}) async-start(bf16[64,32,128]{2,0,1:T(8,128)(2,1)} %bitcast.5), calls=%async_computation | async-start | bytes 1048576 | tf_op jit(solution)/shard_map/all_to_all | solution.py:53
  39.8 11.2 %reshape.173 = bf16[12,256,4,256]{3,2,1,0:T(4,128)(2,1)} reshape(bf16[3072,1024]{1,0:T(8,128)(2,1)} %param.12) | data formatting | bytes 12582912 | tf_op jit(solution)/shard_map/reshape | solution.py:39
  51.1 8.2 %broadcast_multiply_fusion = bf16[12,256,4,256]{3,2,1,0:T(4,128)(2,1)} fusion(bf16[12,256,4,256]{3,2,1,0:T(4,128)(2,1)} %reshape.173, bf16[12,4]{1,0:T(8,128)(2,1)S(1)} %copy.30), kind=kLoop, calls=%fused_computation.4 | loop fusion | flops 3145728 | bytes 12583008 | tf_op jit(solution)/shard_map/mul | solution.py:39
  59.3 4.1 fusion.9
  63.3 1.8 copy.46
  65.7 2.0 copy.48
  69.2 2.2 fusion.10
  72.2 1.4 convolution_add_fusion.2
  75.4 1.9 copy.35
  77.4 23.1 %scatter_fusion = f32[64,1024]{0,1:T(8,128)S(1)} fusion(f32[64,1024]{0,1:T(8,128)S(1)} %copy.34, s32[4096]{0:T(1024)S(1)} %bitcast.214, f32[4096,64]{1,0:T(8,128)} %copy.35), kind=kCustom, calls=%fused_computation.2 | custom fusion | flops 262144 | bytes 3162112 | tf_op jit(solution)/shard_map/scatter-add | solution.py:55
  102.1 1.5 fusion.11
  103.6 1.5 fusion.12
  105.1 14.1 %gather_fusion.1 = f32[4096,64]{1,0:T(8,128)} fusion(f32[64,1024]{0,1:T(8,128)S(1)} %convert_element_type.48, s32[4096]{0:T(1024)S(1)} %copy-done.11), kind=kCustom, calls=%fused_computation.1 | custom fusion | bytes 2113536 | tf_op jit(solution)/shard_map/gather | solution.py:71
  119.2 3.1 copy.37
  122.4 1.5 fusion.2
  143.1 9.9 %all-to-all-start.1 = ((bf16[32,64,1,128]{3,1,2,0:T(8,128)(2,1)}), bf16[32,64,1,128]{3,1,2,0:T(8,128)(2,1)}, u32[]{:S(2)}, u32[]{:S(2)}) async-start(bf16[32,64,1,128]{3,1,2,0:T(8,128)(2,1)} %constant_dynamic-update-slice_fusion), calls=%async_computation.1 | async-start | bytes 1048576 | tf_op jit(solution)/shard_map/all_to_all | solution.py:77
  153.0 5.2 %collective-permute-start.2 = (f32[64,1024]{1,0:T(8,128)}, f32[64,1024]{1,0:T(8,128)S(1)}, u32[]{:S(2)}, u32[]{:S(2)}) collective-permute-start(f32[64,1024]{1,0:T(8,128)} %fusion.11), channel_id=1, source_target_pairs={{8,0},{16,8},{24,16},{32,24},{40,32},{48,40},{56,48},{64,56},{72,6... | collective-permute-start | bytes 786440 | tf_op jit(solution)/shard_map/ppermute | solution.py:12
  158.3 9.5 %collective-permute-done.2 = f32[64,1024]{1,0:T(8,128)S(1)} collective-permute-done((f32[64,1024]{1,0:T(8,128)}, f32[64,1024]{1,0:T(8,128)S(1)}, u32[]{:S(2)}, u32[]{:S(2)}) %collective-permute-start.2) | collective-permute-done | bytes 262176 | tf_op jit(solution)/shard_map/ppermute | solution.py:12
  167.8 5.7 %collective-permute-done.3 = f32[64,1024]{1,0:T(8,128)S(1)} collective-permute-done((f32[64,1024]{1,0:T(8,128)}, f32[64,1024]{1,0:T(8,128)S(1)}, u32[]{:S(2)}, u32[]{:S(2)}) %collective-permute-start.3) | collective-permute-done | bytes 262176 | tf_op jit(solution)/shard_map/ppermute | solution.py:12
  173.5 1.5 fusion
  176.1 1.1 convert_bitcast_fusion
  178.5 1.9 copy.40
  180.4 22.9 %scatter_fusion.1 = f32[64,1024]{0,1:T(8,128)S(1)} fusion(f32[64,1024]{0,1:T(8,128)S(1)} %copy.39, s32[4096]{0:T(1024)S(1)} %bitcast.213, f32[4096,64]{1,0:T(8,128)} %copy.40), kind=kCustom, calls=%fused_computation.3 | custom fusion | flops 262144 | bytes 3162112 | tf_op jit(solution)/shard_map/scatter-add | solution.py:79
  203.3 1.7 convolution_bitcast_fusion
  205.1 2.9 copy.43
  210.0 65.5 %psum.15 = f32[64]{0:T(128)} all-reduce(f32[64]{0:T(128)S(1)} %get-tuple-element.16), channel_id=1, replica_groups=mesh['dom'=32,'hid'=8] {'dom'}, use_global_device_ids=true, to_apply=%region_5.6 | all-reduce | flops 64 | bytes 512 | tf_op jit(solution)/shard_map/psum | solution.py:85
  277.4 176.9 %all-reduce.2.cloned.1.call-done = f32[512,64]{0,1:T(8,128)} async-done(((f32[512,64]{0,1:T(8,128)}), f32[512,64]{0,1:T(8,128)}) %all-reduce.2.cloned.1.call-update) | async-done | bytes 131088 | tf_op jit(solution)/shard_map/psum | solution.py:85
  454.3 1.6 copy.87
  (96 shorter events, 34.4 us)
Async XLA Ops:
  8.0 1.2 copy-start
  10.4 61.8 %collective-permute-start = (bf16[64,1024]{1,0:T(8,128)(2,1)S(1)}, bf16[64,1024]{1,0:T(8,128)(2,1)}, u32[]{:S(2)}, u32[]{:S(2)}) collective-permute-start(bf16[64,1024]{1,0:T(8,128)(2,1)S(1)} %convolution_convert_fusion), channel_id=1, source_target_pairs={{248,0},{0,8},{8,16},{16,24},{24,32},{32,40},{40,48},{48,56},{56,6... | collective-permute-start | bytes 393224 | tf_op jit(solution)/shard_map/ppermute | solution.py:12
  10.5 63.1 %collective-permute-start.1 = (bf16[64,1024]{1,0:T(8,128)(2,1)S(1)}, bf16[64,1024]{1,0:T(8,128)(2,1)S(1)}, u32[]{:S(2)}, u32[]{:S(2)}) collective-permute-start(bf16[64,1024]{1,0:T(8,128)(2,1)S(1)} %convolution_convert_fusion), channel_id=1, source_target_pairs={{8,0},{16,8},{24,16},{32,24},{40,32},{48,40},{56,48},{64,56},{72,6... | collective-permute-start | bytes 393224 | tf_op jit(solution)/shard_map/ppermute | solution.py:12
  33.3 41.0 %all-to-all-start = ((bf16[64,32,128]{2,0,1:T(8,128)(2,1)}), bf16[64,32,128]{2,0,1:T(8,128)(2,1)}, u32[]{:S(2)}, u32[]{:S(2)}) async-start(bf16[64,32,128]{2,0,1:T(8,128)(2,1)} %bitcast.5), calls=%async_computation | async-start | bytes 1048576 | tf_op jit(solution)/shard_map/all_to_all | solution.py:53
  39.8 11.2 %copy-start.14 = (s32[12,4]{0,1:T(4,128)S(1)}, s32[12,4]{0,1:T(4,128)}, u32[]{:S(2)}) copy-start(s32[12,4]{0,1:T(4,128)} %param.13) | copy-start | bytes 580
  65.7 6.5 %copy-start.1 = (bf16[128,8,4,256]{3,1,2,0:T(8,128)(2,1)}, bf16[128,8,4,256]{3,1,2,0:T(8,128)(2,1)S(1)}, u32[]{:S(2)}) copy-start(bf16[128,8,4,256]{3,1,2,0:T(8,128)(2,1)S(1)} %copy.47) | copy-start | bytes 6291460
  65.7 2.0 copy-start.12
  65.7 2.6 copy-start.9
  69.1 4.4 copy-start.3
  69.1 4.4 copy-start.15
  74.3 3.1 copy-start.10
  77.4 23.1 %copy-start.7 = (bf16[64,1024]{0,1:T(8,128)(2,1)S(1)}, bf16[64,1024]{0,1:T(8,128)(2,1)}, u32[]{:S(2)}) copy-start(bf16[64,1024]{0,1:T(8,128)(2,1)} %copy.36) | copy-start | bytes 393220
  100.5 1.7 copy-start.2
  100.5 3.2 copy-start.4
  102.1 3.0 copy-start.11
  122.4 35.9 %copy-start.13 = (s32[1,32,128]{2,1,0:T(8,128)S(1)}, s32[1,32,128]{2,1,0:T(8,128)}, u32[]{:S(2)}) copy-start(s32[1,32,128]{2,1,0:T(8,128)} %param.14) | copy-start | bytes 49156
  122.4 51.1 %copy-start.5 = (bf16[128,8,4,256]{3,1,2,0:T(8,128)(2,1)S(1)}, bf16[128,8,4,256]{3,1,2,0:T(8,128)(2,1)}, u32[]{:S(2)}) copy-start(bf16[128,8,4,256]{3,1,2,0:T(8,128)(2,1)} %copy.46) | copy-start | bytes 6291460
  143.1 33.0 %all-to-all-start.1 = ((bf16[32,64,1,128]{3,1,2,0:T(8,128)(2,1)}), bf16[32,64,1,128]{3,1,2,0:T(8,128)(2,1)}, u32[]{:S(2)}, u32[]{:S(2)}) async-start(bf16[32,64,1,128]{3,1,2,0:T(8,128)(2,1)} %constant_dynamic-update-slice_fusion), calls=%async_computation.1 | async-start | bytes 1048576 | tf_op jit(solution)/shard_map/all_to_all | solution.py:77
  153.0 122.5 %reduce-scatter.4.cloned.1.call-start = ((), (), s32[]{:S(2)}) async-start(), calls=%async_computation.4 | async-start | bytes 2359296
  153.0 14.7 %collective-permute-start.2 = (f32[64,1024]{1,0:T(8,128)}, f32[64,1024]{1,0:T(8,128)S(1)}, u32[]{:S(2)}, u32[]{:S(2)}) collective-permute-start(f32[64,1024]{1,0:T(8,128)} %fusion.11), channel_id=1, source_target_pairs={{8,0},{16,8},{24,16},{32,24},{40,32},{48,40},{56,48},{64,56},{72,6... | collective-permute-start | bytes 786440 | tf_op jit(solution)/shard_map/ppermute | solution.py:12
  158.3 15.2 %collective-permute-start.3 = (f32[64,1024]{1,0:T(8,128)}, f32[64,1024]{1,0:T(8,128)S(1)}, u32[]{:S(2)}, u32[]{:S(2)}) collective-permute-start(f32[64,1024]{1,0:T(8,128)} %fusion.12), channel_id=1, source_target_pairs={{248,0},{0,8},{8,16},{16,24},{24,32},{32,40},{40,48},{48,56},{56,6... | collective-permute-start | bytes 786440 | tf_op jit(solution)/shard_map/ppermute | solution.py:12
  180.4 22.9 %copy-start.8 = (bf16[512,64]{0,1:T(8,128)(2,1)S(1)}, bf16[512,64]{0,1:T(8,128)(2,1)}, u32[]{:S(2)}) copy-start(bf16[512,64]{0,1:T(8,128)(2,1)} %param.11) | copy-start | bytes 196612
  208.0 1.2 copy-start.6
  208.0 246.3 %all-reduce.2.cloned.1.call-start = ((), (), s32[]{:S(2)}) async-start(), calls=%async_computation.3 | async-start | bytes 262144 | tf_op jit(solution)/shard_map/psum | solution.py:85
Sparse Core Ops, SparseCore 0:
  208.1 39.2 reduce-scatter.3
Sparse Core Ops, SparseCore 1:
  211.7 242.6 all-reduce.1
